TPU v7x, 256 devices: a whole 4x4x8 slice. The times are simulated.
256 devices in a mesh: seq: 64 (over x_lo, y, z), sub: 4 (over x_hi, core).
Axes of the slice: x: 4 (x_hi: 2, x_lo: 2; x = x_hi * 2 + x_lo), y: 4, z: 8, core: 2. Of those that a mesh axis runs over, the one named last changes fastest.
Arguments:
- normed: bfloat16 [32768, 2048], P(('seq', 'sub')), as said below
- w_query: bfloat16 [2048, 2048], P(None, 'sub'), as said below
- w_key: bfloat16 [2048, 2048], P(None, 'sub'), as said below
- w_value: bfloat16 [2048, 2048], P(None, 'sub'), may hold values from -0.125 to 0.125
- w_out: bfloat16 [2048, 2048], P('sub'), may hold values from -0.25 to 0.25
- pattern: int32 [16, 128], P('sub'), may hold values from 0 to 127, each once within a row
- slide_lengths: int32 [8], replicated, may hold values from 1 to 160, 256 in all
Outputs:
- mixed: bfloat16 [32768, 2048], P(('seq', 'sub'))
Inputs may be any that keep to these rules, and one draw needn't show every extreme that they name: `pattern`: each row is an ordering of the 128 positions of a block. `slide_lengths`: the slides lie end to end and fill all 256 blocks. `normed`: entries of order one. `w_query`: entries of order 2048 ** -0.5. `w_key`: entries of order 2048 ** -0.5.
All inputs are finite; a program needn't handle non-finite values.
Results may differ from a plain program's by a relative error of at most 0.012.
Values may be sent and summed in bfloat16 or wider, within the bound.
A program may use at most 128 MiB of HBM per device.

v0:
```python
import math
import jax
import jax.numpy as jnp
from jax import lax
from jax.sharding import PartitionSpec as P

HEAD_SIZE = 128
BLOCK = 128
DILATED_KEPT = 16


def slide_count(block_index, slide_ends):
    return jnp.sum((block_index[:, None] >= slide_ends[None, :]).astype(jnp.int32), axis=1)


def shards(normed, w_query, w_key, w_value, w_out, pattern, slide_lengths):
    head_cols = w_query.shape[1]
    nearby_heads = head_cols // HEAD_SIZE
    piece = lax.all_gather(normed, "sub", axis=0, tiled=True)
    outputs = [
        jnp.dot(piece, weight, preferred_element_type=jnp.float32).astype(jnp.bfloat16)
        for weight in (w_query, w_key, w_value)
    ]
    projected = jnp.concatenate(outputs, axis=1)
    queries = projected[:, :head_cols]
    keys_all = projected[:, head_cols : 2 * head_cols]
    values_all = projected[:, 2 * head_cols :]
    span_len = projected.shape[0]
    span_of_blocks = span_len // BLOCK
    my_span = lax.axis_index("seq")
    slide_ends = jnp.cumsum(slide_lengths)
    kept_positions = pattern[:, :DILATED_KEPT]

    def dilate(source):
        blocked = source.reshape(span_of_blocks, BLOCK, nearby_heads, HEAD_SIZE)
        selected_keys = [
            blocked[:, kept_positions[head_index], head_index, :]
            for head_index in range(nearby_heads)
        ]
        return jnp.stack(selected_keys).reshape(
            nearby_heads, span_of_blocks * DILATED_KEPT, HEAD_SIZE
        )

    far_keys, far_values = (
        lax.all_gather(dilate(keys_all), "seq", axis=1, tiled=True),
        lax.all_gather(dilate(values_all), "seq", axis=1, tiled=True),
    )
    distant_count = far_keys.shape[1]
    distant_block = jnp.arange(distant_count, dtype=jnp.int32) // DILATED_KEPT
    distant_slide = slide_count(distant_block, slide_ends)
    far_span = distant_block // span_of_blocks
    row_block = my_span * span_of_blocks + jnp.arange(span_len, dtype=jnp.int32) // BLOCK
    row_slide = slide_count(row_block, slide_ends)
    near_mask = row_slide[:, None] == row_slide[None, :]
    far_mask = (row_slide[:, None] == distant_slide[None, :]) & (far_span != my_span)[None, :]
    scale = 1.0 / math.sqrt(HEAD_SIZE)
    outputs = []
    for head_index in range(nearby_heads):
        columns = slice(head_index * HEAD_SIZE, (head_index + 1) * HEAD_SIZE)
        query_head = queries[:, columns]
        near = (
            jnp.einsum(
                "qd,kd->qk", query_head, keys_all[:, columns], preferred_element_type=jnp.float32
            )
            * scale
        )
        far = (
            jnp.einsum(
                "qd,kd->qk", query_head, far_keys[head_index], preferred_element_type=jnp.float32
            )
            * scale
        )
        near = jnp.where(near_mask, near, -1e30)
        far = jnp.where(far_mask, far, -1e30)
        peak = jnp.maximum(
            jnp.max(near, axis=1, keepdims=True), jnp.max(far, axis=1, keepdims=True)
        )
        near_exp = jnp.exp(near - peak)
        far_exp = jnp.exp(far - peak)
        total = jnp.sum(near_exp, axis=1, keepdims=True) + jnp.sum(far_exp, axis=1, keepdims=True)
        near_weight = (near_exp / total).astype(jnp.bfloat16)
        far_weight = (far_exp / total).astype(jnp.bfloat16)
        context_head = jnp.dot(
            near_weight, values_all[:, columns], preferred_element_type=jnp.float32
        )
        context_head = context_head + jnp.dot(
            far_weight, far_values[head_index], preferred_element_type=jnp.float32
        )
        outputs.append(context_head.astype(jnp.bfloat16))
    context = jnp.concatenate(outputs, axis=1)
    return lax.psum_scatter(
        jnp.dot(context, w_out, preferred_element_type=jnp.float32),
        "sub",
        scatter_dimension=0,
        tiled=True,
    ).astype(jnp.bfloat16)


def solution(mesh):
    placed = (
        P(("seq", "sub"), None),
        P(None, "sub"),
        P(None, "sub"),
        P(None, "sub"),
        P("sub", None),
        P("sub", None),
        P(),
    )
    return jax.shard_map(
        shards, mesh=mesh, in_specs=placed, out_specs=P(("seq", "sub"), None), check_vma=False
    )
```

profile of v0, /device:TPU:1, one launch (start us, length us, event | category | flops | bytes accessed | tf_op | source)
XLA Modules:
  0.0 747.7 jit_solution(3258712888125607824)
XLA Ops:
  6.5 0.7 all-gather.4.cloned.1.call-update
  7.3 0.8 fusion.52
  8.2 34.3 %all-gather.4.cloned.1.call-done = bf16[512,2048]{1,0:T(8,128)(2,1)} async-done(((bf16[128,2048]{1,0:T(8,128)(2,1)}), bf16[512,2048]{1,0:T(8,128)(2,1)}) %all-gather.4.cloned.1.call-update) | async-done | bytes 2097168 | tf_op jit(solution)/shard_map/all_gather | solution.py:19
  42.5 3.5 convolution_convert_fusion.1
  46.0 0.8 copy-done.8
  46.9 0.7 copy.32
  47.6 0.6 gather_fusion.2
  48.2 0.6 gather_fusion.3
  48.8 0.6 gather_fusion
  49.5 0.6 gather_fusion.1
  50.1 0.6 pad_maximum_fusion
  50.8 3.5 convolution_convert_fusion
  54.3 0.8 copy-done.6
  55.2 0.7 copy.40
  55.9 0.6 gather_fusion.4
  56.5 0.6 gather_fusion.5
  57.1 0.6 gather_fusion.6
  57.7 0.6 gather_fusion.7
  58.4 0.6 pad_maximum_fusion.1
  59.5 3.5 convolution_convert_fusion.2
  63.0 2.4 fusion.72
  65.4 1.3 fusion.70
  66.7 1.3 fusion.68
  68.0 1.2 fusion.66
  69.3 238.2 %all-gather.6.cloned.1.call-done = bf16[4,4096,128]{2,1,0:T(8,128)(2,1)} async-done(((bf16[4,64,128]{2,1,0:T(8,128)(2,1)}), bf16[4,4096,128]{2,1,0:T(8,128)(2,1)}) %all-gather.6.cloned.1.call-update) | async-done | bytes 4194320 | tf_op jit(solution)/shard_map/all_gather | solution.py:45
  307.5 3.8 fusion.73
  311.5 3.0 copy-done.1
  314.5 1.3 fusion
  315.8 294.4 %all-gather.8.cloned.1.call-done = bf16[4,4096,128]{2,1,0:T(8,128)(2,1)} async-done(((bf16[4,64,128]{2,1,0:T(8,128)(2,1)}), bf16[4,4096,128]{2,1,0:T(8,128)(2,1)}) %all-gather.8.cloned.1.call-update) | async-done | bytes 4194320 | tf_op jit(solution)/shard_map/all_gather | solution.py:46
  610.1 5.2 fusion.4
  615.3 0.3 fusion.8
  615.7 2.4 fusion.71
  618.2 1.3 fusion.1
  619.6 1.0 copy-done.11
  620.6 2.1 fusion.5
  622.7 0.3 fusion.9
  623.1 2.4 fusion.69
  625.5 1.3 fusion.2
  627.0 2.1 fusion.6
  629.0 0.3 fusion.10
  629.4 2.6 fusion.67
  632.0 1.3 fusion.3
  633.3 0.2 fusion.15
  633.5 2.1 fusion.7
  635.6 0.3 fusion.11
  635.9 3.2 fusion.16
  639.2 99.9 %reduce-scatter.2.cloned.1.call-done = f32[128,2048]{1,0:T(8,128)} async-done(((f32[512,2048]{1,0:T(8,128)}), f32[128,2048]{1,0:T(8,128)}) %reduce-scatter.2.cloned.1.call-update) | async-done | bytes 1048592 | tf_op jit(solution)/shard_map/reduce_scatter | solution.py:91
  739.1 2.1 convert_element_type.71
  (60 shorter events, 1.6 us)
Async XLA Ops:
  6.5 629.4 %copy-start = (bf16[512,2048]{1,0:T(8,128)(2,1)S(1)}, bf16[512,2048]{1,0:T(8,128)(2,1)}, u32[]{:S(2)}) copy-start(bf16[512,2048]{1,0:T(8,128)(2,1)} %param.11) | copy-start | bytes 6291460
  6.5 36.0 %all-gather.4.cloned.1.call-start = ((), (), s32[]{:S(2)}) async-start(), calls=%async_computation.1 | async-start | bytes 2621440 | tf_op jit(solution)/shard_map/all_gather | solution.py:19
  7.3 300.2 %all-gather.6.cloned.1.call-start = ((), (), s32[]{:S(2)}) async-start(), calls=%async_computation.2 | async-start | bytes 4259840 | tf_op jit(solution)/shard_map/all_gather | solution.py:45
  8.1 50.9 %copy-start.12 = (s32[8]{0:T(128)S(1)}, s32[8]{0:T(128)}, u32[]{:S(2)}) copy-start(s32[8]{0:T(128)} %param.13) | copy-start | bytes 100
  46.0 0.8 copy-start.8
  50.7 559.4 %all-gather.8.cloned.1.call-start = ((), (), s32[]{:S(2)}) async-start(), calls=%async_computation.3 | async-start | bytes 4259840 | tf_op jit(solution)/shard_map/all_gather | solution.py:46
  54.3 0.8 copy-start.6
  55.9 9.5 %copy-start.9 = (bf16[512,512]{1,0:T(8,128)(2,1)S(1)}, bf16[512,512]{1,0:T(8,128)(2,1)}, u32[]{:S(2)}) copy-start(bf16[512,512]{1,0:T(8,128)(2,1)} %copy-done.8) | copy-start | bytes 1572868
  59.0 680.0 %reduce-scatter.2.cloned.1.call-start = ((), (), s32[]{:S(2)}) async-start(), calls=%async_computation.4 | async-start | bytes 5242880 | tf_op jit(solution)/shard_map/reduce_scatter | solution.py:91
  63.0 5.0 copy-start.13
  307.5 3.8 copy-start.4
  311.2 3.2 copy-start.1
  610.1 5.2 copy-start.5
  610.1 5.2 copy-start.7
  610.1 5.6 copy-start.10
  610.1 5.6 copy-start.14
  618.1 1.3 copy-start.3
  618.1 2.5 copy-start.11
  625.5 1.3 copy-start.2
Sparse Core Ops, SparseCore 0:
  9.1 33.3 all-gather.3
  50.9 256.5 all-gather.5
  309.3 300.7 all-gather.7
  639.3 99.7 reduce-scatter.1
where the time goes:
time: 748 us
  waiting for transfers between devices  668 us (89%)
  matrix products  43.8 us (6%)
  between operations  13.5 us (2%)
  local copies, waits for them, and re-layouts  12.2 us (2%)
  other arithmetic  10.5 us (1%)
    all_gather x1, waiting for transfers between devices, shards(): lax.all_gather(dilate(values_all), 'seq', axis=1, tiled=True)  294 us
    all_gather x1, waiting for transfers between devices, shards(): lax.all_gather(dilate(keys_all), 'seq', axis=1, tiled=True)  238 us
    reduce_scatter x1, waiting for transfers between devices, shards(): lax.psum_scatter(jnp.dot(context, w_out, preferred_element_type=jnp.float...  99.9 us
    all_gather x1, waiting for transfers between devices, shards(): piece = lax.all_gather(normed, 'sub', axis=0, tiled=True)  34.3 us
  transfers between devices with their start and end apart: 4, of which 4 were waited for; matrix products, arithmetic and copies ran while one was open for 3% of the time, Pallas kernels for 0%

commit v1 on v0

--- a/solution.py
+++ b/solution.py
@@ -41,9 +41,18 @@
             nearby_heads, span_of_blocks * DILATED_KEPT, HEAD_SIZE
         )
 
+    def bring_tails(z, ndim_at):
+        r2 = jnp.concatenate(
+            lax.all_to_all(
+                jnp.stack(lax.axis_size("seq") * [z]), axis_name="seq", split_axis=0, concat_axis=0
+            ),
+            axis=ndim_at,
+        )
+        return r2
+
     far_keys, far_values = (
         lax.all_gather(dilate(keys_all), "seq", axis=1, tiled=True),
-        lax.all_gather(dilate(values_all), "seq", axis=1, tiled=True),
+        bring_tails(dilate(values_all), 1),
     )
     distant_count = far_keys.shape[1]
     distant_block = jnp.arange(distant_count, dtype=jnp.int32) // DILATED_KEPT

time: 748 us -> 479 us (0.64)
  waiting for transfers between devices: 668 us -> 387 us
  starting transfers between devices: 0.13 us -> 10.9 us
    all_gather x1 -> x0, waiting for transfers between devices: 294 us -> none  [shards(): lax.all_gather(dilate(values_all), 'seq', axis=1, tiled=True)]
    all_to_all x0 -> x1, waiting for transfers between devices: none -> 85.2 us  [bring_tails(): lax.all_to_all(jnp.stack(lax.axis_size('seq') * [z]), axis_name='seq', sp...]
    all_gather x1, waiting for transfers between devices: 238 us -> 176 us  [shards(): lax.all_gather(dilate(keys_all), 'seq', axis=1, tiled=True)]
    all_to_all x0 -> x1, starting transfers between devices: none -> 10.6 us  [bring_tails(): lax.all_to_all(jnp.stack(lax.axis_size('seq') * [z]), axis_name='seq', sp...]
    reduce_scatter x1, waiting for transfers between devices: 99.9 us -> 90.6 us  [shards(): lax.psum_scatter(jnp.dot(context, w_out, preferred_element_type=jnp.float...]
  transfers between devices with their start and end apart: 4 -> 4, of which waited for: 4 -> 4; matrix products, arithmetic and copies ran while one was open for 3% -> 5% of each run, Pallas kernels for 0% -> 0%
where the time goes in v1:
time: 479 us
  waiting for transfers between devices  387 us (81%)
  matrix products  41.8 us (9%)
  local copies, waits for them, and re-layouts  16 us (3%)
  between operations  13.5 us (3%)
  starting transfers between devices  10.9 us (2%)
  other arithmetic  9.89 us (2%)
    all_gather x1, waiting for transfers between devices, shards(): lax.all_gather(dilate(keys_all), 'seq', axis=1, tiled=True)  176 us
    reduce_scatter x1, waiting for transfers between devices, shards(): lax.psum_scatter(jnp.dot(context, w_out, preferred_element_type=jnp.float...  90.6 us
    all_to_all x1, waiting for transfers between devices, bring_tails(): lax.all_to_all(jnp.stack(lax.axis_size('seq') * [z]), axis_name='seq', sp...  85.2 us
    all_gather x1, waiting for transfers between devices, shards(): piece = lax.all_gather(normed, 'sub', axis=0, tiled=True)  34.4 us
    dot_general x4, matrix products, shards(): jnp.einsum('qd,kd->qk', query_head, far_keys[head_index], preferred_eleme...  10.9 us
    all_to_all x1, starting transfers between devices, bring_tails(): lax.all_to_all(jnp.stack(lax.axis_size('seq') * [z]), axis_name='seq', sp...  10.6 us
    dot_general x3, matrix products, shards(): jnp.dot(piece, weight, preferred_element_type=jnp.float32)  10.4 us
    dot_general x4, matrix products, shards(): jnp.dot(far_weight, far_values[head_index], preferred_element_type=jnp.fl...  9.63 us
  transfers between devices with their start and end apart: 4, of which 4 were waited for; matrix products, arithmetic and copies ran while one was open for 5% of the time, Pallas kernels for 0%

profile of v1, /device:TPU:1, one launch (start us, length us, event | category | flops | bytes accessed | tf_op | source)
XLA Modules:
  0.0 478.8 jit_solution(9152277677348411887)
XLA Ops:
  6.5 0.7 all-gather.3.cloned.1.call-update
  7.3 0.8 fusion.52
  8.1 34.4 %all-gather.3.cloned.1.call-done = bf16[512,2048]{1,0:T(8,128)(2,1)} async-done(((bf16[128,2048]{1,0:T(8,128)(2,1)}), bf16[512,2048]{1,0:T(8,128)(2,1)}) %all-gather.3.cloned.1.call-update) | async-done | bytes 2097168 | tf_op jit(solution)/shard_map/all_gather | solution.py:19
  42.5 3.5 convolution_convert_fusion
  46.0 0.8 copy-done.8
  46.9 0.7 copy.40
  47.6 0.6 gather_fusion.7
  48.2 0.6 gather_fusion.6
  48.8 0.6 gather_fusion.5
  49.5 0.6 gather_fusion.4
  50.1 3.0 stack.43
  53.1 10.6 %all-to-all-start = ((bf16[64,4,64,128]{3,2,1,0:T(8,128)(2,1)}), bf16[64,4,64,128]{3,2,1,0:T(8,128)(2,1)}, u32[]{:S(2)}, u32[]{:S(2)}) async-start(bf16[64,4,64,128]{3,2,1,0:T(8,128)(2,1)} %stack.43), calls=%async_computation | async-start | bytes 8388608 | tf_op jit(solution)/shard_map/all_to_all | solution.py:46
  63.8 3.5 convolution_convert_fusion.1
  67.3 0.8 copy-done.10
  68.2 0.7 copy.32
  68.9 0.6 gather_fusion.3
  69.5 0.6 gather_fusion.2
  70.1 0.6 gather_fusion.1
  70.7 0.6 gather_fusion
  71.4 0.6 pad_maximum_fusion
  72.0 0.2 reduce-scatter.2.cloned.1.call-start
  72.7 3.5 convolution_convert_fusion.2
  76.2 2.4 fusion.67
  78.6 1.3 fusion.69
  79.8 1.4 fusion.71
  81.2 1.2 fusion.73
  82.4 85.2 %all-to-all-done = bf16[64,4,64,128]{3,2,1,0:T(8,128)(2,1)} async-done(((bf16[64,4,64,128]{3,2,1,0:T(8,128)(2,1)}), bf16[64,4,64,128]{3,2,1,0:T(8,128)(2,1)}, u32[]{:S(2)}, u32[]{:S(2)}) %all-to-all-start) | async-done | bytes 4194336 | tf_op jit(solution)/shard_map/all_to_all | solution.py:46
  167.6 4.8 fusion.66
  172.4 175.7 %all-gather.5.cloned.1.call-done = bf16[4,4096,128]{2,1,0:T(8,128)(2,1)} async-done(((bf16[4,64,128]{2,1,0:T(8,128)(2,1)}), bf16[4,4096,128]{2,1,0:T(8,128)(2,1)}) %all-gather.5.cloned.1.call-update) | async-done | bytes 4194320 | tf_op jit(solution)/shard_map/all_gather | solution.py:54
  348.1 3.8 fusion.68
  352.1 1.3 fusion.3
  353.4 2.5 fusion.7
  356.0 0.3 fusion.11
  356.3 2.4 fusion.70
  358.9 1.3 fusion.2
  360.2 2.3 fusion.6
  362.5 0.3 fusion.10
  362.9 2.4 fusion.72
  365.5 1.3 fusion.1
  366.8 2.5 fusion.5
  369.4 0.3 fusion.9
  369.7 2.4 fusion.74
  372.3 1.3 fusion
  373.6 2.3 fusion.4
  375.9 0.3 fusion.8
  376.3 3.2 fusion.16
  379.5 90.6 %reduce-scatter.2.cloned.1.call-done = f32[128,2048]{1,0:T(8,128)} async-done(((f32[512,2048]{1,0:T(8,128)}), f32[128,2048]{1,0:T(8,128)}) %reduce-scatter.2.cloned.1.call-update) | async-done | bytes 1048592 | tf_op jit(solution)/shard_map/reduce_scatter | solution.py:100
  470.1 2.1 convert_element_type.71
  (63 shorter events, 1.7 us)
Async XLA Ops:
  6.5 369.7 %copy-start = (bf16[512,2048]{1,0:T(8,128)(2,1)S(1)}, bf16[512,2048]{1,0:T(8,128)(2,1)}, u32[]{:S(2)}) copy-start(bf16[512,2048]{1,0:T(8,128)(2,1)} %param.11) | copy-start | bytes 6291460
  6.5 36.0 %all-gather.3.cloned.1.call-start = ((), (), s32[]{:S(2)}) async-start(), calls=%async_computation.2 | async-start | bytes 2621440 | tf_op jit(solution)/shard_map/all_gather | solution.py:19
  46.0 0.8 copy-start.8
  53.1 19.1 %copy-start.13 = (s32[8]{0:T(128)S(1)}, s32[8]{0:T(128)}, u32[]{:S(2)}) copy-start(s32[8]{0:T(128)} %param.13) | copy-start | bytes 100
  53.1 114.5 %all-to-all-start = ((bf16[64,4,64,128]{3,2,1,0:T(8,128)(2,1)}), bf16[64,4,64,128]{3,2,1,0:T(8,128)(2,1)}, u32[]{:S(2)}, u32[]{:S(2)}) async-start(bf16[64,4,64,128]{3,2,1,0:T(8,128)(2,1)} %stack.43), calls=%async_computation | async-start | bytes 8388608 | tf_op jit(solution)/shard_map/all_to_all | solution.py:46
  63.7 284.4 %all-gather.5.cloned.1.call-start = ((), (), s32[]{:S(2)}) async-start(), calls=%async_computation.3 | async-start | bytes 4259840 | tf_op jit(solution)/shard_map/all_gather | solution.py:54
  67.3 0.8 copy-start.10
  68.9 9.7 %copy-start.11 = (bf16[512,512]{1,0:T(8,128)(2,1)S(1)}, bf16[512,512]{1,0:T(8,128)(2,1)}, u32[]{:S(2)}) copy-start(bf16[512,512]{1,0:T(8,128)(2,1)} %copy-done.10) | copy-start | bytes 1572868
  72.0 398.1 %reduce-scatter.2.cloned.1.call-start = ((), (), s32[]{:S(2)}) async-start(), calls=%async_computation.4 | async-start | bytes 5242880 | tf_op jit(solution)/shard_map/reduce_scatter | solution.py:100
  76.2 5.0 %copy-start.14 = (bf16[512,512]{1,0:T(8,128)(2,1)}, bf16[512,512]{1,0:T(8,128)(2,1)S(1)}, u32[]{:S(2)}) copy-start(bf16[512,512]{1,0:T(8,128)(2,1)S(1)} %convolution_convert_fusion.2) | copy-start | bytes 1572868
  348.1 3.8 copy-start.3
  351.9 1.5 copy-start.7
  353.4 2.6 copy-start.9
  353.4 2.9 copy-start.12
  353.4 2.9 copy-start.15
  356.3 2.4 copy-start.2
  358.7 1.5 copy-start.6
  362.9 2.4 copy-start.1
  365.3 1.5 copy-start.5
  372.1 1.5 copy-start.4
Sparse Core Ops, SparseCore 0:
  9.1 33.3 all-gather.2
  72.2 275.9 all-gather.4
  379.6 90.4 reduce-scatter.1
